TPU v7x, 32 devices: a whole 2x2x4 slice. The times are simulated.
32 devices in a mesh: grp: 4 (over y, core), py: 4 (over z), pz: 2 (over x).
Axes of the slice: x: 2, y: 2, z: 4, core: 2. Of those that a mesh axis runs over, the one named last changes fastest.
Arguments:
- velocity: float32 [3, 192, 64, 256], P(None, 'grp', 'py', 'pz'), may hold values from -6 to 6
- spectral_weight: float32 [32, 32, 32, 2, 32, 32], P('py', 'pz', None, None, 'grp'), may hold values from -24 to 24
- lift_weight: float32 [3, 32], replicated, may hold values from -3.5 to 3.5
- mixing_weight: float32 [32, 32], replicated, may hold values from -1 to 1
- project_weight: float32 [32, 3], replicated, may hold values from -1 to 1
Outputs:
- velocity_next: float32 [3, 192, 64, 256], P(None, 'grp', 'py', 'pz')
- grad_spectral: float32 [32, 32, 32, 2, 32, 32], P('py', 'pz', None, None, 'grp')
- grad_mixing: float32 [32, 32], replicated
- mean_loss: float32 [], replicated
All inputs are finite; a program needn't handle non-finite values.
Results may differ from a plain program's by a relative error of at most 0.006.
Values may be sent and summed in bfloat16 or wider, within the bound.
No kernel may reach another device: no remote copies, remote signals or barrier semaphores. Data moves between devices by JAX's collectives and lax.ppermute only.
A program may use at most 576 MiB of HBM per device.

v0:
```python
import math

import jax
import jax.numpy as jnp
from jax import lax
from jax.sharding import PartitionSpec as P

MX = 32
MY = 32
MZ = 32


time_step = 0.1
viscosity = 0.6
precise = lax.Precision.HIGHEST


def with_halo(cells, sides, width):
    for axis, dim in sides:
        count = lax.axis_size(axis)
        ends = count - 1
        head = lax.slice_in_dim(cells, 0, width, axis=dim)
        tail = lax.slice_in_dim(cells, cells.shape[dim] - width, cells.shape[dim], axis=dim)
        cells = jnp.concatenate(
            [
                lax.ppermute(tail, axis, [(i, (i + 1) % count) for i in range(ends)]),
                cells,
                lax.ppermute(head, axis, [((i + 1) % count, i) for i in range(ends)]),
            ],
            axis=dim,
        )
    return cells


def contract(form, left, right):
    return jnp.einsum(form, left, right, precision=precise)


def tables(length, mode_count, signed):
    points = jnp.arange(length, dtype=jnp.int32)
    frequency = jnp.arange(mode_count, dtype=jnp.int32)
    if signed:
        frequency = jnp.where(frequency < mode_count // 2, frequency, frequency - mode_count)
    phase_index = frequency[:, None] * points[None, :] % length
    angles = phase_index.astype(jnp.float32) * (2.0 * math.pi / length)
    return (jnp.cos(angles), jnp.sin(angles))


def forward_x(field_value):
    cosine_table, sine_table = tables(field_value.shape[1], MX, False)
    real_part = contract("cxyz,kx->ckyz", field_value, cosine_table)
    imag_part = -contract("cxyz,kx->ckyz", field_value, sine_table)
    return jnp.stack([real_part, imag_part])


def forward_y(spectrum):
    values = spectrum.astype(jnp.float32)
    cosine_table, sine_table = tables(values.shape[3], MY, True)
    real_part = contract("cmyz,ky->cmkz", values[0], cosine_table) + contract(
        "cmyz,ky->cmkz", values[1], sine_table
    )
    imag_part = contract("cmyz,ky->cmkz", values[1], cosine_table) - contract(
        "cmyz,ky->cmkz", values[0], sine_table
    )
    return jnp.stack([real_part, imag_part])


def forward_z(spectrum):
    values = spectrum.astype(jnp.float32)
    cosine_table, sine_table = tables(values.shape[4], MZ, True)
    real_part = contract("cmkz,jz->cmkj", values[0], cosine_table) + contract(
        "cmkz,jz->cmkj", values[1], sine_table
    )
    imag_part = contract("cmkz,jz->cmkj", values[1], cosine_table) - contract(
        "cmkz,jz->cmkj", values[0], sine_table
    )
    return jnp.stack([real_part, imag_part])


def inverse_z(spectrum, length):
    values = spectrum.astype(jnp.float32)
    cosine_table, sine_table = tables(length, MZ, True)
    real_part = (
        contract("cmkj,jz->cmkz", values[0], cosine_table)
        - contract("cmkj,jz->cmkz", values[1], sine_table)
    ) / length
    imag_part = (
        contract("cmkj,jz->cmkz", values[1], cosine_table)
        + contract("cmkj,jz->cmkz", values[0], sine_table)
    ) / length
    return jnp.stack([real_part, imag_part])


def inverse_y(spectrum, length):
    values = spectrum.astype(jnp.float32)
    cosine_table, sine_table = tables(length, MY, True)
    real_part = (
        contract("cmkz,ky->cmyz", values[0], cosine_table)
        - contract("cmkz,ky->cmyz", values[1], sine_table)
    ) / length
    imag_part = (
        contract("cmkz,ky->cmyz", values[1], cosine_table)
        + contract("cmkz,ky->cmyz", values[0], sine_table)
    ) / length
    return jnp.stack([real_part, imag_part])


def inverse_x(spectrum, length):
    values = spectrum.astype(jnp.float32)
    cosine_table, sine_table = tables(length, MX, False)
    doubling = jnp.where(jnp.arange(MX, dtype=jnp.int32) == 0, 1.0, 2.0).astype(jnp.float32)[
        :, None
    ]
    return (
        contract("ckyz,kx->cxyz", values[0], cosine_table * doubling)
        - contract("ckyz,kx->cxyz", values[1], sine_table * doubling)
    ) / length


def mix_modes(spectrum, weights):
    real_part = contract("cabk,abkco->oabk", spectrum[0], weights[:, :, :, 0]) - contract(
        "cabk,abkco->oabk", spectrum[1], weights[:, :, :, 1]
    )
    imag_part = contract("cabk,abkco->oabk", spectrum[0], weights[:, :, :, 1]) + contract(
        "cabk,abkco->oabk", spectrum[1], weights[:, :, :, 0]
    )
    return jnp.stack([real_part, imag_part])


def grad_modes(spectrum, back_modes):
    real_part = contract("cabk,oabk->abkco", spectrum[0], back_modes[0]) + contract(
        "cabk,oabk->abkco", spectrum[1], back_modes[1]
    )
    imag_part = contract("cabk,oabk->abkco", spectrum[0], back_modes[1]) - contract(
        "cabk,oabk->abkco", spectrum[1], back_modes[0]
    )
    return jnp.stack([real_part, imag_part], axis=3)


def tendency(padded):
    center = padded[:, 1:-1, 1:-1, 1:-1]
    shifted_up = (padded[:, 2:, 1:-1, 1:-1], padded[:, 1:-1, 2:, 1:-1], padded[:, 1:-1, 1:-1, 2:])
    shifted_down = (
        padded[:, :-2, 1:-1, 1:-1],
        padded[:, 1:-1, :-2, 1:-1],
        padded[:, 1:-1, 1:-1, :-2],
    )
    advection = (
        center[0:1] * (shifted_up[0] - shifted_down[0])
        + center[1:2] * (shifted_up[1] - shifted_down[1])
        + center[2:3] * (shifted_up[2] - shifted_down[2])
    )
    laplacian = (
        shifted_up[0]
        + shifted_down[0]
        + shifted_up[1]
        + shifted_down[1]
        + shifted_up[2]
        + shifted_down[2]
        - 6.0 * center
    )
    return -0.5 * advection + viscosity * laplacian


def coarsen(field_value):
    shape_now = field_value.shape
    blocks = field_value.reshape(
        shape_now[0], shape_now[1] // 2, 2, shape_now[2] // 2, 2, shape_now[3] // 2, 2
    )
    return jnp.mean(blocks, axis=(2, 4, 6))


def local(velocity, spectral_weight, lift_weight, mixing_weight, project_weight):
    groups = lax.axis_size("grp")
    trainer = lax.axis_index("grp") == groups - 1

    def on_trainer(function, operand):
        return lax.cond(
            trainer,
            function,
            lambda operand_value: jax.tree.map(jnp.zeros_like, function(operand_value)),
            operand,
        )

    def opening(snapshot):
        return forward_x(contract("ic,ixyz->cxyz", lift_weight, snapshot))

    weights_full = lax.all_gather(spectral_weight, "grp", axis=4, tiled=True)
    field_start = jnp.where(trainer, jnp.zeros_like(velocity), velocity)
    first_coarse = coarsen(field_start)

    def advance(current, anchor, keep_share, step_share):
        padded = with_halo(
            current.astype(jnp.bfloat16), (("grp", 1), ("py", 2), ("pz", 3)), 1
        ).astype(current.dtype)

        def update(operands):
            padded_value, current_value = operands
            return keep_share * anchor + step_share * (
                current_value + time_step * tendency(padded_value)
            )

        return lax.cond(
            trainer, lambda operands: jnp.zeros_like(operands[1]), update, (padded, current)
        )

    section_one = advance(field_start, field_start, 0.0, 1.0)
    section_two = advance(section_one, field_start, 0.75, 0.25)
    section_three = advance(section_two, field_start, 1.0 / 3.0, 2.0 / 3.0)
    velocity_next = jnp.where(trainer, velocity, section_three)
    second_coarse = coarsen(section_three)
    first_all, second_all = (
        lax.all_gather(first_coarse, "grp", axis=1, tiled=True),
        lax.all_gather(second_coarse, "grp", axis=1, tiled=True),
    )
    extent = (groups - 1) * first_coarse.shape[1]
    before = first_all[:, :extent]
    target = second_all[:, :extent]
    height_cells = first_coarse.shape[2] * lax.axis_size("py")
    depth_cells = first_coarse.shape[3] * lax.axis_size("pz")
    cell_count = extent * height_cells * depth_cells
    spectrum_x = on_trainer(opening, before)
    spectrum_x = lax.all_to_all(spectrum_x, "py", split_axis=2, concat_axis=3, tiled=True)
    spectrum_y = on_trainer(forward_y, spectrum_x)
    spectrum_y = lax.all_to_all(spectrum_y, "pz", split_axis=3, concat_axis=4, tiled=True)
    spectrum = on_trainer(lambda values: forward_z(values), spectrum_y)

    def middle(operands):
        values, weights = operands
        mixed_modes = mix_modes(values, weights).astype(jnp.bfloat16)
        return inverse_z(mixed_modes, depth_cells).astype(jnp.bfloat16)

    inner_z = on_trainer(middle, (spectrum, weights_full))
    inner_z = lax.all_to_all(inner_z, "pz", split_axis=4, concat_axis=3, tiled=True)
    inner_y = on_trainer(
        lambda values: inverse_y(values, height_cells).astype(jnp.bfloat16), inner_z
    )
    inner_y = lax.all_to_all(inner_y, "py", split_axis=3, concat_axis=2, tiled=True)

    def opening_close(operands):
        values, before_value = operands
        lifted = contract("ic,ixyz->cxyz", lift_weight, before_value)
        pre_activation = inverse_x(values, extent) + contract(
            "co,cxyz->oxyz", mixing_weight, lifted
        )
        sigmoid_gate = jax.nn.sigmoid(pre_activation)
        hidden = pre_activation * sigmoid_gate
        projected = contract("ci,cxyz->ixyz", project_weight, hidden)
        return (lifted, pre_activation, sigmoid_gate, projected)

    lifted, pre_activation, sigmoid_gate, projected = on_trainer(opening_close, (inner_y, before))

    def closing(operands):
        lifted_value, pre_value, gate_value, projected_value, before_value, target_value = operands
        residual = before_value + projected_value - target_value
        grad_pre = (
            contract("ci,ixyz->cxyz", project_weight, residual)
            * gate_value
            * (1.0 + pre_value * (1.0 - gate_value))
        )
        mix_part = contract("cxyz,oxyz->co", lifted_value, grad_pre)
        loss_term = 0.5 * jnp.sum(residual * residual)
        return (forward_x(grad_pre).astype(jnp.bfloat16), mix_part, loss_term)

    back_x, mix_term, loss_term = on_trainer(
        closing, (lifted, pre_activation, sigmoid_gate, projected, before, target)
    )
    back_x = lax.all_to_all(back_x, "py", split_axis=2, concat_axis=3, tiled=True)
    back_y = on_trainer(lambda values: forward_y(values).astype(jnp.bfloat16), back_x)
    back_y = lax.all_to_all(back_y, "pz", split_axis=3, concat_axis=4, tiled=True)
    local_modes = spectrum.shape[2]
    wave_index = lax.axis_index("py") * local_modes + jnp.arange(local_modes, dtype=jnp.int32)
    factor = jnp.where(wave_index == 0, 1.0, 2.0).astype(jnp.float32) / cell_count
    back_modes = on_trainer(
        lambda values: forward_z(values) * factor[None, None, :, None, None], back_y
    )
    grad_term = on_trainer(
        lambda operands: grad_modes(operands[0], operands[1]), (spectrum, back_modes)
    )
    grad_spectral = lax.psum_scatter(
        grad_term.astype(jnp.bfloat16), "grp", scatter_dimension=4, tiled=True
    ).astype(jnp.float32)
    mix_total, loss_total = lax.psum((mix_term, loss_term), ("grp", "py", "pz"))
    return (velocity_next, grad_spectral, mix_total / cell_count, loss_total / cell_count)


def solution(mesh):
    return jax.shard_map(
        local,
        mesh=mesh,
        in_specs=(
            P(None, "grp", "py", "pz"),
            P("py", "pz", None, None, "grp", None),
            P(),
            P(),
            P(),
        ),
        out_specs=(P(None, "grp", "py", "pz"), P("py", "pz", None, None, "grp", None), P(), P()),
        check_vma=False,
    )
```

profile of v0, /device:TPU:0, one launch (start us, length us, event | category | flops | bytes accessed | tf_op | source)
XLA Modules:
  0.0 2104.4 jit_solution(6305804738349208032)
XLA Ops:
  9.5 76.8 %reshape.94 = f32[3,24,2,8,2,64,2]{6,5,4,3,2,1,0:T(8,128)} reshape(f32[3,48,16,128]{3,2,1,0:T(8,128)S(1)} %get-tuple-element.331) | data formatting | bytes 2359296 | tf_op jit(solution)/shard_map/reshape | solution.py:167
  86.3 24.6 %reduce_sum.27 = f32[3,24,8,64]{3,2,1,0:T(8,128)S(1)} reduce(f32[3,24,2,8,2,64,2]{6,5,4,3,2,1,0:T(8,128)} %reshape.94, f32[]{:T(128)} %constant.287.clone.1), dimensions={2,4,6}, to_apply=%region_6.7 | reduce | flops 258048 | bytes 1327108 | tf_op jit(solution)/shard_map/reduce_sum | solution.py:170
  110.9 18.8 all_gather.9
  166.3 94.0 %all-to-all-done = f32[4,1,262144]{2,1,0:T(1,128)} async-done(((f32[4,1,262144]{2,1,0:T(1,128)}), f32[4,1,262144]{2,1,0:T(1,128)}, u32[]{:S(2)}, u32[]{:S(2)}) %all-to-all-start) | async-done | bytes 4194336 | tf_op jit(solution)/shard_map/all_to_all | solution.py:223
  260.8 15.3 reduce.8
  331.4 47.3 %all-to-all-done.1 = f32[2,1,524288]{2,1,0:T(1,128)} async-done(((f32[2,1,524288]{2,1,0:T(1,128)}), f32[2,1,524288]{2,1,0:T(1,128)}, u32[]{:S(2)}, u32[]{:S(2)}) %all-to-all-start.1) | async-done | bytes 4194336 | tf_op jit(solution)/shard_map/all_to_all | solution.py:225
  378.7 17.0 reduce.9
  428.2 383.5 %all-gather.2.cloned.1.call-done = f32[8,16,32,2,32,32]{5,4,3,2,1,0:T(8,128)} async-done(((f32[8,16,32,2,8,32]{5,4,3,2,1,0:T(8,128)}), f32[8,16,32,2,32,32]{5,4,3,2,1,0:T(8,128)}) %all-gather.2.cloned.1.call-update) | async-done | bytes 33554448 | tf_op jit(solution)/shard_map/all_gather | solution.py:188
  812.6 12.5 copy.218
  845.5 20.2 all-to-all-done.2
  871.5 16.2 copy.290
  922.7 18.5 collective-permute-done.3
  961.1 18.9 conditional.13
  988.2 17.6 collective-permute-start.8
  1020.0 20.6 conditional.14
  1042.0 87.2 %collective-permute-start.12 = (bf16[3,1,16,128]{3,2,1,0:T(8,128)(2,1)S(1)}, bf16[3,1,16,128]{3,2,1,0:T(8,128)(2,1)S(1)}, u32[]{:S(2)}, u32[]{:S(2)}) collective-permute-start(bf16[3,1,16,128]{3,2,1,0:T(8,128)(2,1)S(1)} %get-tuple-element.372), channel_id=1, source_target_pairs={{0,8},{8,16},{16,24},{1,9},{9,17},{17,25},{2,10},{10,18},{18,26},{... | collective-permute-start | bytes 36872 | tf_op jit(solution)/shard_map/ppermute | solution.py:26
  1153.6 20.2 conditional.15
  1173.8 76.8 %reshape.95 = f32[3,24,2,8,2,64,2]{6,5,4,3,2,1,0:T(8,128)} reshape(f32[3,48,16,128]{3,2,1,0:T(8,128)S(1)} %get-tuple-element.394) | data formatting | bytes 2359296 | tf_op jit(solution)/shard_map/reshape | solution.py:167
  1250.6 23.3 %reduce_sum.28 = f32[3,24,8,64]{3,2,1,0:T(8,128)S(1)} reduce(f32[3,24,2,8,2,64,2]{6,5,4,3,2,1,0:T(8,128)} %reshape.95, f32[]{:T(128)} %constant.287.clone.1), dimensions={2,4,6}, to_apply=%region_19.20 | reduce | flops 258048 | bytes 1327108 | tf_op jit(solution)/shard_map/reduce_sum | solution.py:170
  1274.0 16.2 all_gather.11
  1305.2 21.7 %conditional.21 = (f32[32,72,8,64]{1,0,3,2:T(8,128)}, f32[32,72,8,64]{1,3,2,0:T(8,128)}, f32[32,72,8,64]{1,3,2,0:T(8,128)}, f32[3,72,8,64]{1,0,3,2:T(4,128)S(1)}) conditional(s32[]{:T(128)} %convert_element_type.119, () %tuple.121, (f32[3,32]{1,0:T(4,128)S(1)}, f32[3,72,8,64]{3,2,0,1:T(8,128)S(1)}, bf16[2,32,4,8,8,64]{5,4,2,3,1,0:T(8,128)(2,1)}, ...), branch_computations={%region_17.18_spmd, %region_18.19_spmd} | conditional | flops 1452192768 | bytes 65738684 | solution.py:178
  1356.6 48.7 %all-to-all-done.4 = bf16[4,2,131072]{2,1,0:T(2,128)(2,1)S(1)} async-done(((bf16[4,2,131072]{2,1,0:T(2,128)(2,1)}), bf16[4,2,131072]{2,1,0:T(2,128)(2,1)S(1)}, u32[]{:S(2)}, u32[]{:S(2)}) %all-to-all-start.4) | async-done | bytes 2097184 | tf_op jit(solution)/shard_map/all_to_all | solution.py:268
  1414.6 20.4 conditional.23
  1450.5 25.0 %all-to-all-done.5 = bf16[2,2,262144]{2,1,0:T(2,128)(2,1)S(1)} async-done(((bf16[2,2,262144]{2,1,0:T(2,128)(2,1)}), bf16[2,2,262144]{2,1,0:T(2,128)(2,1)S(1)}, u32[]{:S(2)}, u32[]{:S(2)}) %all-to-all-start.5) | async-done | bytes 2097184 | tf_op jit(solution)/shard_map/all_to_all | solution.py:270
  1491.3 21.3 %conditional.25 = (bf16[8,16,32,2,32,32]{5,4,2,1,0,3:T(8,128)(2,1)}) conditional(s32[]{:T(128)} %convert_element_type.119, () %tuple.113, (f32[2,32,8,16,32]{1,4,3,2,0:T(8,128)}, f32[2,32,8,16,32]{1,4,3,2,0:T(8,128)}) %tuple.128), branch_computations={%region_27.28_spmd, %region_28.29_spmd} | conditional | flops 41943040 | bytes 65011720 | solution.py:178
  1491.3 21.1 %broadcast.321 = bf16[8,16,32,2,32,32]{5,4,2,1,0,3:T(8,128)(2,1)} broadcast(bf16[]{:T(256)} %constant.651), dimensions={} | broadcast | bytes 16777218 | tf_op jit(solution)/shard_map/broadcast.127
  1512.6 101.2 %copy_bitcast_fusion.20 = bf16[32,8,16,32,2,32]{5,4,3,2,1,0:T(2,128)(2,1)} fusion(bf16[8,16,32,2,32,32]{5,4,2,1,0,3:T(8,128)(2,1)} %get-tuple-element.402), kind=kLoop, calls=%fused_computation.396 | loop fusion | bytes 33554432
  1613.7 54.6 %reshape.132 = bf16[32,262144]{1,0:T(8,128)(2,1)} reshape(bf16[32,8,16,32,2,32]{5,4,3,2,1,0:T(2,128)(2,1)} %copy_bitcast_fusion.20) | data formatting | bytes 33554432
  1671.2 264.0 %all-reduce = (f32[32,32]{1,0:T(8,128)S(1)}, f32[]{:T(128)}) all-reduce(f32[32,32]{1,0:T(8,128)S(1)} %copy.240, f32[]{:T(128)} %get-tuple-element.170), channel_id=1, replica_groups=mesh['grp'=4,'py'=4,'pz'=2] {'grp','py','pz'}, use_global_device_ids=true, to_apply=%region_30.31 | all-reduce | flops 1025 | bytes 8200 | tf_op jit(solution)/shard_map/psum | solution.py:283
  1936.5 81.6 %reduce-scatter.4.cloned.1.call-done = bf16[8,262144]{1,0:T(8,128)(2,1)} async-done(((bf16[32,262144]{1,0:T(8,128)(2,1)}), bf16[8,262144]{1,0:T(8,128)(2,1)}) %reduce-scatter.4.cloned.1.call-update) | async-done | bytes 4194320
  2024.2 33.5 %reshape.133 = bf16[8,8,16,32,2,32]{5,4,3,2,1,0:T(2,128)(2,1)} reshape(bf16[2097152]{0:T(1024)(128)(2,1)} %reshape.134) | data formatting | bytes 8388608
  2057.6 38.6 %copy_convert_fusion.1 = f32[8,16,32,2,8,32]{5,4,3,2,1,0:T(8,128)} fusion(bf16[8,16,32,2,8,32]{5,3,2,1,0,4:T(2,128)(2,1)} %bitcast.396), kind=kLoop, calls=%fused_computation.397 | loop fusion | flops 2097152 | bytes 12582912 | tf_op jit(solution)/shard_map/convert_element_type | solution.py:282
  (169 shorter events, 448.2 us)
Async XLA Ops:
  7.2 804.5 %all-gather.2.cloned.1.call-start = ((), (), s32[]{:S(2)}) async-start(), calls=%async_computation.7 | async-start | bytes 167772160 | tf_op jit(solution)/shard_map/all_gather | solution.py:188
  9.5 76.8 %copy-start = (f32[3,48,16,128]{3,2,1,0:T(8,128)}, f32[3,48,16,128]{3,2,1,0:T(8,128)S(1)}, u32[]{:S(2)}) copy-start(f32[3,48,16,128]{3,2,1,0:T(8,128)S(1)} %get-tuple-element.331) | copy-start | bytes 3538948
  110.9 18.9 copy-start.23
  160.9 99.4 %all-to-all-start = ((f32[4,1,262144]{2,1,0:T(1,128)}), f32[4,1,262144]{2,1,0:T(1,128)}, u32[]{:S(2)}, u32[]{:S(2)}) async-start(f32[4,1,262144]{2,1,0:T(1,128)} %reshape.136), calls=%async_computation | async-start | bytes 8388608 | tf_op jit(solution)/shard_map/all_to_all | solution.py:223
  325.8 52.9 %all-to-all-start.1 = ((f32[2,1,524288]{2,1,0:T(1,128)}), f32[2,1,524288]{2,1,0:T(1,128)}, u32[]{:S(2)}, u32[]{:S(2)}) async-start(f32[2,1,524288]{2,1,0:T(1,128)} %reshape.138), calls=%async_computation.1 | async-start | bytes 8388608 | tf_op jit(solution)/shard_map/all_to_all | solution.py:225
  836.3 29.4 %all-to-all-start.2 = ((bf16[2,2,262144]{2,1,0:T(2,128)(2,1)}), bf16[2,2,262144]{2,1,0:T(2,128)(2,1)S(1)}, u32[]{:S(2)}, u32[]{:S(2)}) async-start(bf16[2,2,262144]{2,1,0:T(2,128)(2,1)} %reshape.140), calls=%async_computation.2 | async-start | bytes 4194304 | tf_op jit(solution)/shard_map/all_to_all | solution.py:234
  840.2 4.3 collective-permute-start.1
  841.5 3.9 collective-permute-start
  910.8 379.4 %all-to-all-start.3 = ((bf16[4,2,131072]{2,1,0:T(2,128)(2,1)}), bf16[4,2,131072]{2,1,0:T(2,128)(2,1)}, u32[]{:S(2)}, u32[]{:S(2)}) async-start(bf16[4,2,131072]{2,1,0:T(2,128)(2,1)} %reshape.142), calls=%async_computation.3 | async-start | bytes 4194304 | tf_op jit(solution)/shard_map/all_to_all | solution.py:238
  915.5 25.7 %collective-permute-start.3 = (bf16[3,50,1,128]{3,1,2,0:T(8,128)(2,1)S(1)}, bf16[3,50,1,128]{3,1,2,0:T(8,128)(2,1)S(1)}, u32[]{:S(2)}, u32[]{:S(2)}) collective-permute-start(bf16[3,50,1,128]{3,1,2,0:T(8,128)(2,1)S(1)} %copy.304), channel_id=1, source_target_pairs={{2,0},{4,2},{6,4},{3,1},{5,3},{7,5},{10,8},{12,10},{14,12},{11,9},... | collective-permute-start | bytes 115208 | tf_op jit(solution)/shard_map/ppermute | solution.py:28
  916.8 33.1 %collective-permute-start.2 = (bf16[3,50,1,128]{3,1,2,0:T(8,128)(2,1)S(1)}, bf16[3,50,1,128]{3,1,2,0:T(8,128)(2,1)S(1)}, u32[]{:S(2)}, u32[]{:S(2)}) collective-permute-start(bf16[3,50,1,128]{3,1,2,0:T(8,128)(2,1)S(1)} %copy.303), channel_id=1, source_target_pairs={{0,2},{2,4},{4,6},{1,3},{3,5},{5,7},{8,10},{10,12},{12,14},{9,11},... | collective-permute-start | bytes 115208 | tf_op jit(solution)/shard_map/ppermute | solution.py:26
  950.1 5.9 collective-permute-start.5
  951.4 6.0 collective-permute-start.4
  980.1 4.3 collective-permute-start.7
  981.4 3.9 collective-permute-start.6
  986.9 20.6 collective-permute-start.9
  988.2 20.7 collective-permute-start.8
  1009.0 5.9 collective-permute-start.11
  1010.3 6.0 collective-permute-start.10
  1040.6 89.4 %copy-start.9 = (f32[3,48,16,128]{3,2,1,0:T(8,128)}, f32[3,48,16,128]{3,2,1,0:T(8,128)S(1)}, u32[]{:S(2)}) copy-start(f32[3,48,16,128]{3,2,1,0:T(8,128)S(1)} %get-tuple-element.393) | copy-start | bytes 3538948
  1040.7 88.5 %collective-permute-start.13 = (bf16[3,1,16,128]{3,2,1,0:T(8,128)(2,1)S(1)}, bf16[3,1,16,128]{3,2,1,0:T(8,128)(2,1)S(1)}, u32[]{:S(2)}, u32[]{:S(2)}) collective-permute-start(bf16[3,1,16,128]{3,2,1,0:T(8,128)(2,1)S(1)} %get-tuple-element.373), channel_id=1, source_target_pairs={{8,0},{16,8},{24,16},{9,1},{17,9},{25,17},{10,2},{18,10},{26,18},{... | collective-permute-start | bytes 36872 | tf_op jit(solution)/shard_map/ppermute | solution.py:28
  1042.0 88.0 %collective-permute-start.12 = (bf16[3,1,16,128]{3,2,1,0:T(8,128)(2,1)S(1)}, bf16[3,1,16,128]{3,2,1,0:T(8,128)(2,1)S(1)}, u32[]{:S(2)}, u32[]{:S(2)}) collective-permute-start(bf16[3,1,16,128]{3,2,1,0:T(8,128)(2,1)S(1)} %get-tuple-element.372), channel_id=1, source_target_pairs={{0,8},{8,16},{16,24},{1,9},{9,17},{17,25},{2,10},{10,18},{18,26},{... | collective-permute-start | bytes 36872 | tf_op jit(solution)/shard_map/ppermute | solution.py:26
  1133.4 7.7 collective-permute-start.15
  1134.7 7.9 collective-permute-start.14
  1142.6 5.9 collective-permute-start.17
  1143.9 6.0 collective-permute-start.16
  1173.8 76.9 %copy-start.11 = (f32[3,48,16,128]{3,2,1,0:T(8,128)}, f32[3,48,16,128]{3,2,1,0:T(8,128)S(1)}, u32[]{:S(2)}) copy-start(f32[3,48,16,128]{3,2,1,0:T(8,128)S(1)} %get-tuple-element.394) | copy-start | bytes 3538948
  1296.0 9.2 copy-start.24
  1296.0 9.2 copy-start.25
  1349.9 55.4 %all-to-all-start.4 = ((bf16[4,2,131072]{2,1,0:T(2,128)(2,1)}), bf16[4,2,131072]{2,1,0:T(2,128)(2,1)S(1)}, u32[]{:S(2)}, u32[]{:S(2)}) async-start(bf16[4,2,131072]{2,1,0:T(2,128)(2,1)} %reshape.144), calls=%async_computation.4 | async-start | bytes 4194304 | tf_op jit(solution)/shard_map/all_to_all | solution.py:268
  1446.7 28.8 %all-to-all-start.5 = ((bf16[2,2,262144]{2,1,0:T(2,128)(2,1)}), bf16[2,2,262144]{2,1,0:T(2,128)(2,1)S(1)}, u32[]{:S(2)}, u32[]{:S(2)}) async-start(bf16[2,2,262144]{2,1,0:T(2,128)(2,1)} %reshape.146), calls=%async_computation.5 | async-start | bytes 4194304 | tf_op jit(solution)/shard_map/all_to_all | solution.py:270
  1450.4 567.6 %reduce-scatter.4.cloned.1.call-start = ((), (), s32[]{:S(2)}) async-start(), calls=%async_computation.8 | async-start | bytes 20971520
  (13 other events, 51.7 us)
Sparse Core Ops, SparseCore 0:
  9.5 802.1 all-gather.1
  1668.5 349.5 reduce-scatter.3
where the time goes:
time: 2110 us; the launch traced here: 2100 us
  waiting for transfers between devices  741 us (35%)
  local copies, waits for them, and re-layouts  642 us (30%)
  blocking collectives  299 us (14%)
  starting transfers between devices  175 us (8%)
  other arithmetic  165 us (8%)
  loops' own time  64.9 us (3%)
    all_gather x1, waiting for transfers between devices, local(): weights_full = lax.all_gather(spectral_weight, 'grp', axis=4, tiled=True)  383 us
    unnamed x52, local copies, waits for them, and re-layouts  284 us
    psum x1, blocking collectives, local(): mix_total, loss_total = lax.psum((mix_term, loss_term), ('grp', 'py', 'pz'))  264 us
    reshape x2, local copies, waits for them, and re-layouts, coarsen(): field_value.reshape(shape_now[0], shape_now[1] // 2, 2, shape_now[2] // 2...  154 us
    ppermute x9, starting transfers between devices, with_halo(): lax.ppermute(tail, axis, [(i, (i + 1) % count) for i in range(ends)])  134 us
    all_to_all x1, waiting for transfers between devices, local(): lax.all_to_all(spectrum_x, 'py', split_axis=2, concat_axis=3, tiled=True)  94 us
    unnamed x3, waiting for transfers between devices  82.3 us
    another operation x17, local copies, waits for them, and re-layouts  76.9 us
  transfers between devices with their start and end apart: 26, of which 19 were waited for; matrix products, arithmetic and copies ran while one was open for 19% of the time, Pallas kernels for 0%

commit v1 on v0

--- a/solution.py
+++ b/solution.py
@@ -2,7 +2,10 @@
 
 import jax
 import jax.numpy as jnp
+import numpy as np
 from jax import lax
+from jax.experimental import pallas as pl
+from jax.experimental.pallas import tpu as pltpu
 from jax.sharding import PartitionSpec as P
 
 MX = 32
@@ -170,7 +173,7 @@
     return jnp.mean(blocks, axis=(2, 4, 6))
 
 
-def local(velocity, spectral_weight, lift_weight, mixing_weight, project_weight):
+def general(velocity, spectral_weight, lift_weight, mixing_weight, project_weight):
     groups = lax.axis_size("grp")
     trainer = lax.axis_index("grp") == groups - 1
 
@@ -284,7 +287,646 @@
     return (velocity_next, grad_spectral, mix_total / cell_count, loss_total / cell_count)
 
 
+ALL = ("grp", "py", "pz")
+C = 32
+LANES = 128
+VMEM = 60 * 1024 * 1024
+
+
+def dot(left, right, dims=((1,), (0,))):
+    return lax.dot_general(
+        left, right, (dims, ((), ())), precision=precise, preferred_element_type=jnp.float32
+    )
+
+
+def dot16(left, right, dims=((1,), (0,))):
+    return lax.dot_general(
+        left.astype(jnp.bfloat16),
+        right.astype(jnp.bfloat16),
+        (dims, ((), ())),
+        preferred_element_type=jnp.float32,
+    )
+
+
+def call(kernel, out_shape, scratch=(), **kwargs):
+    return pl.pallas_call(
+        kernel,
+        out_shape=out_shape,
+        scratch_shapes=list(scratch),
+        compiler_params=pltpu.CompilerParams(vmem_limit_bytes=VMEM),
+        **kwargs,
+    )
+
+
+def shape_of(*dims, kind=jnp.float32):
+    return jax.ShapeDtypeStruct(dims, kind)
+
+
+def signed(count):
+    index = np.arange(count)
+    return np.where(index < count // 2, index, index - count)
+
+
+def turn(frequency, point, length):
+    angle = 2.0 * np.pi * ((frequency * point) % length) / length
+    return np.cos(angle), np.sin(angle)
+
+
+class Plan:
+    def __init__(self, groups, rows, cols, cells):
+        self.G, self.PY, self.PZ = groups, rows, cols
+        self.cells = cells
+        self.nx, self.ny, self.nz = cells
+        self.cx, self.cy, self.cz = (n // 2 for n in cells)
+        self.X = (groups - 1) * self.cx
+        self.Y = self.cy * rows
+        self.Z = self.cz * cols
+        self.D = groups * rows * cols
+        self.W = rows * cols
+        self.a = MX // rows
+        self.b = MY // cols
+        self.kz = MZ // self.W
+        self.no = C // groups
+        self.ky = 4
+        self.t = self.b // self.ky
+        self.XP = -(-self.X // 16) * 16
+        self.Q = self.XP * self.no // LANES
+        self.count = self.X * self.Y * self.Z
+
+    def tables(self):
+        f32 = np.float32
+        G, PY, PZ, D, W = self.G, self.PY, self.PZ, self.D, self.W
+        kx = np.arange(MX)
+        fy, fz = signed(MY), signed(MZ)
+        out = {}
+        c, s = turn(kx[:, None], np.arange(self.X)[None, :], self.X)
+        out["xm"] = np.concatenate([c, -s], 0).astype(f32)
+        tz = np.zeros((PZ, 2, 2, LANES, LANES))
+        for p in range(PZ):
+            z = p * self.cz + np.arange(self.cz)
+            c, s = turn(fz[None, :], z[:, None], self.Z)
+            for h in range(2):
+                for k, v in enumerate((c, s)):
+                    tz[p, k, h, h * self.cz : (h + 1) * self.cz] = np.tile(v, (1, self.ky))
+        out["tz"] = tz.astype(f32)
+        tiles = MY // self.ky
+        cy = np.zeros((PY, 2, tiles * self.cy, LANES))
+        for p in range(PY):
+            y = p * self.cy + np.arange(self.cy)
+            c, s = turn(fy[:, None], y[None, :], self.Y)
+            for k, v in enumerate((c, s)):
+                v = v.reshape(tiles, self.ky, self.cy).transpose(0, 2, 1)
+                cy[p, k] = np.repeat(v, MZ, axis=2).reshape(tiles * self.cy, LANES)
+        out["cy"] = cy.astype(f32)
+        d = np.arange(D)
+        g, py, pz = d // W, (d // PZ) % PY, d % PZ
+        yrow = py * self.cy + g * PZ + pz
+        ky_of = np.arange(MY).reshape(PZ, self.t, self.ky)
+        c, s = turn(fy[None, :], yrow[:, None], self.Y)
+        eye = np.eye(self.kz)
+
+        def block(rr, ri, ir, ii):
+            m = np.zeros((D, 2, self.kz, PZ, self.t, 2, self.ky, self.kz))
+            for i, row in enumerate(((rr, ri), (ir, ii))):
+                for o, v in enumerate(row):
+                    v = v[:, ky_of]
+                    m[:, o, :, :, :, i] = np.einsum("dpty,kl->dkptyl", v, eye)
+            n = D * 2 * self.kz
+            return m.reshape(n, PZ * LANES)
+
+        out["m1"] = block(c, s, -s, c).astype(f32)
+        out["m2"] = block(-s, c, -c, -s).astype(f32)
+
+        def back(rr, ri, ir, ii):
+            m = np.zeros((D, 2, self.kz, PZ, self.t, 2, self.ky, self.kz))
+            for i, row in enumerate(((rr, ri), (ir, ii))):
+                for o, v in enumerate(row):
+                    v = v[:, ky_of]
+                    m[:, i, :, :, :, o] = np.einsum("dpty,kl->dkptyl", v, eye)
+            return m.reshape(D * 2 * self.kz, PZ * LANES)
+
+        out["n1"] = back(c, -s, s, c).astype(f32)
+        out["n2"] = back(-s, -c, c, -s).astype(f32)
+        weight = np.where(kx == 0, 1.0, 2.0)
+        c, s = turn(kx[:, None], np.arange(self.X)[None, :], self.X)
+        eye = np.eye(self.no)
+
+        def wide(v):
+            m = np.zeros((MX, self.no, self.XP, self.no))
+            m[:, :, : self.X] = np.einsum("kx,op->koxp", v, eye)
+            return m.reshape(MX * self.no, self.XP * self.no).astype(f32)
+
+        inverse = weight[:, None] / self.X
+        forward = weight[:, None] / self.count
+        out["cx"], out["sx"] = wide(c * inverse), wide(s * inverse)
+        out["cxt"], out["sxt"] = wide(c * forward), wide(s * forward)
+        c, s = turn(fz[:, None], np.arange(self.Z)[None, :], self.Z)
+
+        def zrows(first, second, scale):
+            v = np.stack([first, second]).reshape(2, W, self.kz, self.Z).transpose(1, 0, 2, 3)
+            return (v * scale).reshape(W * 2 * self.kz, self.Z).astype(f32)
+
+        out["zi"] = zrows(c, -s, 1.0 / (self.Y * self.Z))
+        out["zf"] = zrows(c, -s, 1.0)
+        pairs = np.zeros((2, LANES, LANES))
+        for h in range(2):
+            z = np.arange(LANES)
+            pairs[h, z, h * self.cz + z // 2] = 0.125
+        out["pairs"] = pairs.astype(f32)
+        return out
+
+
+def coarse_rows(ref, plan, row):
+    total = None
+    for dx in range(2):
+        for dy in range(2):
+            start = dx * plan.ny + 2 * row + dy
+            part = ref[pl.ds(start, 3 * plan.cx, stride=2 * plan.ny), :]
+            total = part if total is None else total + part
+    return total
+
+
+def put_faces(ref, plan, xlo, xhi):
+    n = plan.ny
+    for i in range(3):
+        base = i * plan.nx * n
+        xlo[i * n : (i + 1) * n, :] = ref[base : base + n, :]
+        xhi[i * n : (i + 1) * n, :] = ref[base + (plan.nx - 1) * n : base + plan.nx * n, :]
+
+
+def lane_ids(rows):
+    return lax.broadcasted_iota(jnp.int32, (rows, LANES), 1)
+
+
+def put_z(plane, i, x, plan, zlo, zhi):
+    n = plan.ny
+    rows = slice(i * n, (i + 1) * n)
+    here = lane_ids(n) == x
+    zlo[rows, :] = jnp.where(here, pltpu.roll(plane, x, 1), zlo[rows, :])
+    zhi[rows, :] = jnp.where(here, pltpu.roll(plane, x + 1, 1), zhi[rows, :])
+
+
+def opening_kernel(plan, u, pairs, coarse, xlo, xhi, ylo, yhi, zlo, zhi):
+    count = 3 * plan.nx
+    ylo[...] = u[pl.ds(0, count, stride=plan.ny), :]
+    yhi[...] = u[pl.ds(plan.ny - 1, count, stride=plan.ny), :]
+    put_faces(u, plan, xlo, xhi)
+    for q in range(plan.cy // 2):
+        total = dot(coarse_rows(u, plan, 2 * q), pairs[0]) + dot(
+            coarse_rows(u, plan, 2 * q + 1), pairs[1]
+        )
+        coarse[:, q * LANES : (q + 1) * LANES] = total
+    zlo[...] = jnp.zeros_like(zlo)
+    zhi[...] = jnp.zeros_like(zhi)
+
+    def body(step, carry):
+        for k in range(4):
+            x = step * 4 + k
+            for i in range(3):
+                start = pl.multiple_of((i * plan.nx + x) * plan.ny, plan.ny)
+                put_z(u[pl.ds(start, plan.ny), :], i, x, plan, zlo, zhi)
+        return carry
+
+    lax.fori_loop(0, plan.nx // 4, body, 0)
+
+
+def stage_kernel(plan, keep, share, last, *refs):
+    if last:
+        flag, u, anchor, hxlo, hxhi, hylo, hyhi, hzlo, hzhi, pairs, out, both, hold = refs
+    else:
+        u, anchor, hxlo, hxhi, hylo, hyhi, hzlo, hzhi, out, xlo, xhi, ylo, yhi, zlo, zhi = refs
+        zlo[...] = jnp.zeros_like(zlo)
+        zhi[...] = jnp.zeros_like(zhi)
+    n = plan.ny
+    lanes = lane_ids(n)
+    rows = lax.broadcasted_iota(jnp.int32, (n, LANES), 0)
+
+    def plane_of(ref, i, x):
+        return ref[pl.ds(pl.multiple_of((i * plan.nx + x) * n, n), n), :]
+
+    def one(x):
+        center = [plane_of(u, i, x) for i in range(3)]
+        for i in range(3):
+            c = center[i]
+            r = i * plan.nx + x
+            face = slice(i * n, (i + 1) * n)
+            down = jnp.where(x == 0, hxlo[face, :], plane_of(u, i, jnp.maximum(x - 1, 0)))
+            up = jnp.where(
+                x == plan.nx - 1, hxhi[face, :], plane_of(u, i, jnp.minimum(x + 1, plan.nx - 1))
+            )
+            ydown = jnp.where(rows == 0, hylo[pl.ds(r, 1), :], pltpu.roll(c, 1, 0))
+            yup = jnp.where(rows == n - 1, hyhi[pl.ds(r, 1), :], pltpu.roll(c, n - 1, 0))
+            zdown = jnp.where(
+                lanes == 0, pltpu.roll(hzlo[face, :], LANES - x, 1), pltpu.roll(c, 1, 1)
+            )
+            zup = jnp.where(
+                lanes == LANES - 1,
+                pltpu.roll(hzhi[face, :], LANES - 1 - x, 1),
+                pltpu.roll(c, LANES - 1, 1),
+            )
+            advection = (
+                center[0] * (up - down) + center[1] * (yup - ydown) + center[2] * (zup - zdown)
+            )
+            laplacian = up + down + yup + ydown + zup + zdown - 6.0 * c
+            new = share * (c + time_step * (viscosity * laplacian - 0.5 * advection))
+            if keep:
+                new = new + keep * plane_of(anchor, i, x)
+            out[pl.ds(pl.multiple_of(r * n, n), n), :] = new
+            if not last:
+                ylo[pl.ds(r, 1), :] = new[0:1]
+                yhi[pl.ds(r, 1), :] = new[n - 1 : n]
+                put_z(new, i, x, plan, zlo, zhi)
+
+    def body(step, carry):
+        for k in range(4):
+            one(step * 4 + k)
+        return carry
+
+    lax.fori_loop(0, plan.nx // 4, body, 0)
+    if last:
+        for row in range(plan.cy):
+            first = coarse_rows(anchor, plan, row)
+            gap = first - coarse_rows(out, plan, row)
+            hold[row] = dot(first, pairs[0]) + dot(gap, pairs[1])
+        both[...] = hold[...].astype(jnp.bfloat16)
+
+        @pl.when(flag[0] > 0)
+        def _():
+            out[...] = anchor[...]
+    else:
+        put_faces(out, plan, xlo, xhi)
+
+
+def spectrum_kernel(plan, cg, xm, tz, cy, hold):
+    tiles = MY // plan.ky
+    for i in range(3):
+        field = jnp.concatenate(
+            [cg[g, i * plan.cx : (i + 1) * plan.cx, :] for g in range(plan.G - 1)], axis=0
+        )
+        f = dot(xm[...], field)
+        real, imag = [], []
+        for y in range(plan.cy):
+            part = f[:, (y // 2) * LANES : (y // 2 + 1) * LANES]
+            cosine, sine = dot(part, tz[0, y % 2]), dot(part, tz[1, y % 2])
+            real.append(cosine[:MX] + sine[MX:])
+            imag.append(cosine[MX:] - sine[:MX])
+        for t in range(tiles):
+            sum_re = sum_im = 0.0
+            for y in range(plan.cy):
+                row = t * plan.cy + y
+                c, s = cy[0, row : row + 1, :], cy[1, row : row + 1, :]
+                sum_re = sum_re + c * real[y] + s * imag[y]
+                sum_im = sum_im + c * imag[y] - s * real[y]
+            owner, inner = t // plan.t, t % plan.t
+            for p in range(plan.PY):
+                rows = slice(p * plan.a, (p + 1) * plan.a)
+                for k, value in enumerate((sum_re, sum_im)):
+                    at = ((i * 2 + k) * plan.t + inner) * plan.a
+                    hold[p * plan.PZ + owner, at : at + plan.a, :] = value[rows]
+
+
+def halves(value):
+    high = value.astype(jnp.bfloat16)
+    return high, (value - high.astype(jnp.float32)).astype(jnp.bfloat16)
+
+
+def mode_block(plan, rows_ref, w, t, a):
+    n = plan.ky * plan.kz
+    lanes = lax.broadcasted_iota(jnp.int32, (n, n * 2 * plan.no), 1) // (2 * plan.no)
+    here = lanes == lax.broadcasted_iota(jnp.int32, (n, n * 2 * plan.no), 0)
+    parts = [
+        jnp.where(here, rows_ref[w, k, pl.ds(t * plan.a + a, 1), :], 0.0) for k in range(2)
+    ]
+    return jnp.concatenate(parts, axis=0)
+
+
+def mix_kernel(plan, received, coef, weights, rows_out, out, hold):
+    a = pl.program_id(0)
+    n = plan.ky * plan.kz
+    wide = n * 2 * plan.no
+
+    @pl.when(a == 0)
+    def _():
+        total = received[0]
+        for source in range(1, plan.W):
+            total = total + received[source]
+        high, low = halves(total)
+        lane_in = lax.broadcasted_iota(jnp.int32, (LANES, wide), 0)
+        mode = lax.broadcasted_iota(jnp.int32, (LANES, wide), 1) // (2 * plan.no)
+        step = plan.t * plan.a
+        for w in range(plan.W):
+            want = (mode // plan.kz) * MZ + w * plan.kz + mode % plan.kz
+            pick = jnp.where(lane_in == want, 1.0, 0.0).astype(jnp.bfloat16)
+            spread = dot16(high, pick) + dot16(low, pick)
+            for k in range(2):
+                rows = 0.0
+                for j in range(6):
+                    at = k * 6 + j
+                    rows = rows + coef[at : at + 1, :] * spread[j * step : (j + 1) * step]
+                rows_out[w, k] = rows
+
+    at = pl.multiple_of(a * plan.no, plan.no)
+    for w in range(plan.W):
+        parts = []
+        for t in range(plan.t):
+            block = weights[
+                0, t * plan.ky : (t + 1) * plan.ky, w * plan.kz : (w + 1) * plan.kz
+            ].reshape(wide, C)
+            high, low = halves(mode_block(plan, rows_out, w, t, a))
+            weight, rest = halves(block)
+            both = dot16(jnp.concatenate([high, low], axis=0), weight)
+            parts.append(both[: 2 * n] + both[2 * n :] + dot16(high, rest))
+        mixed = jnp.concatenate(parts, axis=0).T
+        for g in range(plan.G):
+            hold[g * plan.W + w, pl.ds(at, plan.no), :] = mixed[g * plan.no : (g + 1) * plan.no]
+
+    @pl.when(a == plan.a - 1)
+    def _():
+        out[...] = hold[...].astype(jnp.bfloat16)
+
+
+def inverse_kernel(plan, received, m1, m2, cx, sx, out, hold):
+    rows = []
+    for p in range(plan.PY):
+        cols = []
+        for q in range(plan.PZ):
+            total = 0.0
+            for g in range(plan.G):
+                total = total + received[g * plan.W + p * plan.PZ + q].astype(jnp.float32)
+            cols.append(total)
+        rows.append(jnp.concatenate(cols, axis=1))
+    modes = jnp.concatenate(rows, axis=0)
+    nt = ((1,), (1,))
+    value = dot(dot(m1[...], modes, nt), cx[...]) + dot(dot(m2[...], modes, nt), sx[...])
+    for q in range(plan.Q):
+        hold[:, q * 8 : (q + 1) * 8, :] = value[:, q * LANES : (q + 1) * LANES].reshape(
+            plan.D, 8, LANES
+        )
+    out[...] = hold[...].astype(jnp.bfloat16)
+
+
+def point_kernel(plan, received, both, zi, zf, mixc, projc, out, taken, hold):
+    W, G, no = plan.W, plan.G, plan.no
+    per = LANES // no
+    taken[...] = received[...].astype(jnp.float32)
+    tn, nt = ((0,), (0,)), ((1,), (1,))
+    moments = [[0.0] * 3 for _ in range(G)]
+    loss = 0.0
+    for q in range(plan.Q):
+        x = slice(q * per, (q + 1) * per)
+        before = [both[0, i, x] for i in range(3)]
+        gap = [both[1, i, x] for i in range(3)]
+        pres, gates = [], []
+        shown = [0.0] * 3
+        for g in range(G):
+            modes = taken[g * W : (g + 1) * W, q * 8 : (q + 1) * 8, :].reshape(W * 8, LANES)
+            pre = dot(modes, zi[...], tn).reshape(per, no, LANES)
+            for i in range(3):
+                pre = pre + mixc[g * 3 + i] * before[i]
+            gate = jax.nn.sigmoid(pre)
+            hidden = pre * gate
+            for i in range(3):
+                shown[i] = shown[i] + jnp.sum(projc[g * 3 + i] * hidden, axis=1, keepdims=True)
+            pres.append(pre)
+            gates.append(gate)
+        residual = [shown[i] + gap[i] for i in range(3)]
+        loss = loss + sum(jnp.sum(r * r, axis=0) for r in residual)
+        for g in range(G):
+            slope = sum(projc[g * 3 + i] * residual[i] for i in range(3))
+            slope = slope * gates[g] * (1.0 + pres[g] * (1.0 - gates[g]))
+            for i in range(3):
+                moments[g][i] = moments[g][i] + jnp.sum(slope * before[i], axis=0)
+            modes = dot(zf[...], slope.reshape(LANES, LANES), nt)
+            hold[g * W : (g + 1) * W, q * 8 : (q + 1) * 8, :] = modes.reshape(W, 8, LANES)
+    lanes = lane_ids(no)
+    tile = jnp.zeros((no, LANES), jnp.float32)
+
+    def place(tile, value, index):
+        high = value.astype(jnp.bfloat16).astype(jnp.float32)
+        tile = jnp.where(lanes == index, high, tile)
+        return jnp.where(lanes == index + LANES // 2, value - high, tile)
+
+    for g in range(G):
+        for i in range(3):
+            tile = place(tile, jnp.sum(moments[g][i], axis=1, keepdims=True), g * 3 + i)
+    tile = place(tile, jnp.broadcast_to(jnp.sum(loss, axis=1, keepdims=True), (no, 1)), G * 3)
+    hold[:, plan.Q * 8 :, :] = jnp.broadcast_to(tile[None], (plan.D, no, LANES))
+    out[...] = hold[...].astype(jnp.bfloat16)
+
+
+def forward_kernel(plan, received, cxt, sxt, n1, n2, out, stats, taken):
+    taken[...] = received[...].astype(jnp.float32)
+    stats[...] = jnp.sum(taken[:, plan.Q * 8 :, :], axis=0)
+    first = second = 0.0
+    nt = ((1,), (1,))
+    for q in range(plan.Q):
+        rows = taken[:, q * 8 : (q + 1) * 8, :].reshape(plan.D * 8, LANES)
+        cols = slice(q * LANES, (q + 1) * LANES)
+        first = first + dot(cxt[:, cols], rows, nt)
+        second = second + dot(sxt[:, cols], rows, nt)
+    modes = (dot(first, n1[...]) + dot(second, n2[...])).astype(jnp.bfloat16)
+    size = plan.a * plan.no
+    for p in range(plan.PY):
+        for q in range(plan.PZ):
+            tile = modes[p * size : (p + 1) * size, q * LANES : (q + 1) * LANES]
+            for g in range(plan.G):
+                out[g * plan.W + p * plan.PZ + q] = tile
+
+
+def grad_kernel(plan, rows_ref, received, out, taken):
+    a = pl.program_id(0)
+    n = plan.ky * plan.kz
+
+    @pl.when(a == 0)
+    def _():
+        taken[...] = received[...].astype(jnp.float32)
+
+    at = pl.multiple_of(a * plan.no, plan.no)
+    for w in range(plan.W):
+        back = jnp.concatenate(
+            [taken[g * plan.W + w, pl.ds(at, plan.no), :] for g in range(plan.G)], axis=0
+        ).T
+        for t in range(plan.t):
+            block = dot16(
+                mode_block(plan, rows_ref, w, t, a), back[t * 2 * n : (t + 1) * 2 * n], ((0,), (0,))
+            )
+            out[0, t * plan.ky : (t + 1) * plan.ky, w * plan.kz : (w + 1) * plan.kz] = (
+                block.reshape(plan.ky, plan.kz, 2, plan.no, C)
+            )
+
+
+def halos(faces, plan):
+    xlo, xhi, ylo, yhi, zlo, zhi = faces
+    out = []
+    for low, high, axis, count in (
+        (xlo, xhi, "grp", plan.G - 1),
+        (ylo, yhi, "py", plan.PY),
+        (zlo, zhi, "pz", plan.PZ),
+    ):
+        up = [(i, i + 1) for i in range(count - 1)]
+        out.append(lax.ppermute(high, axis, up))
+        out.append(lax.ppermute(low, axis, [(j, i) for i, j in up]))
+    return out
+
+
+def everyone(plan, velocity, spectral_weight, lift_weight, mixing_weight, project_weight):
+    tables = plan.tables()
+    G, W, D = plan.G, plan.W, plan.D
+    n = plan.ny
+    group = lax.axis_index("grp")
+    flag = (group == G - 1).astype(jnp.int32)[None]
+    cells = 3 * plan.nx * n
+    field = velocity.reshape(cells, LANES)
+    faces_shape = [shape_of(3 * n, LANES)] * 2 + [shape_of(3 * plan.nx, LANES)] * 2
+    faces_shape = faces_shape + [shape_of(3 * n, LANES)] * 2
+    full = shape_of(cells, LANES)
+
+    def bind(kernel, *args):
+        return lambda *refs: kernel(plan, *args, *refs)
+
+    coarse, *faces = call(
+        bind(opening_kernel), [shape_of(3 * plan.cx, plan.cy * plan.cz)] + faces_shape
+    )(field, tables["pairs"])
+    edges = halos(faces, plan)
+
+    gathered = lax.all_gather(coarse, "grp", axis=0)
+    tz = lax.dynamic_index_in_dim(jnp.asarray(tables["tz"]), lax.axis_index("pz"), 0, False)
+    cy = lax.dynamic_index_in_dim(jnp.asarray(tables["cy"]), lax.axis_index("py"), 0, False)
+    lines = 6 * plan.t * plan.a
+    spectra = call(
+        bind(spectrum_kernel),
+        shape_of(W, lines, LANES),
+    )(gathered, tables["xm"], tz, cy)
+    spectra = lax.all_to_all(spectra, ("py", "pz"), 0, 0, tiled=True)
+
+    lift = lax.dynamic_slice_in_dim(lift_weight, group * plan.no, plan.no, axis=1)
+    zero = jnp.zeros_like(lift)
+    first = jnp.concatenate([lift, zero], axis=1)
+    second = jnp.concatenate([zero, lift], axis=1)
+    coef = jnp.stack(
+        [jnp.stack([first, -second], 1), jnp.stack([second, first], 1)]
+    ).reshape(12, 2 * plan.no)
+    wide = plan.ky * plan.kz * 2 * plan.no
+    coef = jnp.tile(coef, (1, plan.ky * plan.kz))
+    lift_rows, mixed = pl.pallas_call(
+        bind(mix_kernel),
+        grid=(plan.a,),
+        in_specs=[
+            pl.BlockSpec((W, lines, LANES), lambda i: (0, 0, 0)),
+            pl.BlockSpec((12, wide), lambda i: (0, 0)),
+            pl.BlockSpec((1, plan.b, MZ, 2, plan.no, C), lambda i: (i, 0, 0, 0, 0, 0)),
+        ],
+        out_specs=[
+            pl.BlockSpec((W, 2, plan.t * plan.a, wide), lambda i: (0, 0, 0, 0)),
+            pl.BlockSpec((D, plan.a * plan.no, LANES), lambda i: (0, 0, 0)),
+        ],
+        out_shape=[
+            shape_of(W, 2, plan.t * plan.a, wide),
+            shape_of(D, plan.a * plan.no, LANES, kind=jnp.bfloat16),
+        ],
+        scratch_shapes=[pltpu.VMEM((D, plan.a * plan.no, LANES), jnp.float32)],
+        compiler_params=pltpu.CompilerParams(vmem_limit_bytes=VMEM),
+    )(spectra, coef, spectral_weight)
+    mixed = lax.all_to_all(mixed, ALL, 0, 0, tiled=True)
+
+    tall = plan.Q * 8
+    inner = call(
+        bind(inverse_kernel),
+        shape_of(D, tall, LANES, kind=jnp.bfloat16),
+        [pltpu.VMEM((D, tall, LANES), jnp.float32)],
+    )(mixed, tables["m1"], tables["m2"], tables["cx"], tables["sx"])
+    inner = lax.all_to_all(inner, ALL, 0, 0, tiled=True)
+
+    one, *faces = call(bind(stage_kernel, 0.0, 1.0, False), [full] + faces_shape)(
+        field, field, *edges
+    )
+    edges = halos(faces, plan)
+    two, *faces = call(bind(stage_kernel, 0.75, 0.25, False), [full] + faces_shape)(
+        one, field, *edges
+    )
+    edges = halos(faces, plan)
+    both_shape = (plan.cy, 3 * plan.cx, LANES)
+    smem = pl.BlockSpec(memory_space=pltpu.SMEM)
+    vmem = pl.BlockSpec(memory_space=pltpu.VMEM)
+    three, both = call(
+        bind(stage_kernel, 1.0 / 3.0, 2.0 / 3.0, True),
+        [full, shape_of(*both_shape, kind=jnp.bfloat16)],
+        [pltpu.VMEM(both_shape, jnp.float32)],
+        in_specs=[smem] + [vmem] * 9,
+    )(flag, two, field, *edges, tables["pairs"])
+    velocity_next = three.reshape(velocity.shape)
+
+    both = lax.all_to_all(both, ("grp", "pz"), 0, 0, tiled=True)
+    both = both.reshape(G, plan.PZ, 3, plan.cx, 2, plan.cz)[: G - 1].astype(jnp.float32)
+    both = both.transpose(4, 2, 0, 3, 1, 5).reshape(2, 3, plan.X, plan.Z)
+    both = jnp.pad(both, ((0, 0), (0, 0), (0, plan.XP - plan.X), (0, 0)))[:, :, :, None, :]
+
+    def column(value):
+        value = value.reshape(3, G, plan.no).transpose(1, 0, 2).reshape(G * 3, plan.no, 1)
+        return jnp.broadcast_to(value, (G * 3, plan.no, LANES))
+
+    mixc = column(contract("ic,co->io", lift_weight, mixing_weight))
+    projc = column(project_weight.T)
+    back = call(
+        bind(point_kernel),
+        shape_of(D, tall + 8, LANES, kind=jnp.bfloat16),
+        [pltpu.VMEM((D, tall, LANES), jnp.float32), pltpu.VMEM((D, tall + 8, LANES), jnp.float32)],
+    )(inner, both, tables["zi"], tables["zf"], mixc, projc)
+    back = lax.all_to_all(back, ALL, 0, 0, tiled=True)
+
+    modes, stats = call(
+        bind(forward_kernel),
+        [shape_of(D, plan.a * plan.no, LANES, kind=jnp.bfloat16), shape_of(plan.no, LANES)],
+        [pltpu.VMEM((D, tall + 8, LANES), jnp.float32)],
+    )(back, tables["cxt"], tables["sxt"], tables["n1"], tables["n2"])
+    modes = lax.all_to_all(modes, ALL, 0, 0, tiled=True)
+
+    grad_spectral = pl.pallas_call(
+        bind(grad_kernel),
+        grid=(plan.a,),
+        in_specs=[
+            pl.BlockSpec((W, 2, plan.t * plan.a, wide), lambda i: (0, 0, 0, 0)),
+            pl.BlockSpec((D, plan.a * plan.no, LANES), lambda i: (0, 0, 0)),
+        ],
+        out_specs=pl.BlockSpec((1, plan.b, MZ, 2, plan.no, C), lambda i: (i, 0, 0, 0, 0, 0)),
+        out_shape=shape_of(*spectral_weight.shape),
+        scratch_shapes=[pltpu.VMEM((D, plan.a * plan.no, LANES), jnp.float32)],
+        compiler_params=pltpu.CompilerParams(vmem_limit_bytes=VMEM),
+    )(lift_rows, modes)
+
+    half = LANES // 2
+    stats = (stats[:, :half] + stats[:, half:]) / plan.count
+    moments = stats[:, : G * 3].reshape(plan.no, G, 3).transpose(2, 1, 0).reshape(3, C)
+    grad_mixing = contract("ic,io->co", lift_weight, moments)
+    return velocity_next, grad_spectral, grad_mixing, 0.5 * stats[0, G * 3]
+
+
+def plan_of(mesh, velocity):
+    groups, rows, cols = (mesh.shape[name] for name in ALL)
+    plan = Plan(groups, rows, cols, velocity.shape[1:])
+    fits = (
+        plan.nz == LANES
+        and plan.Z == LANES
+        and plan.W * plan.kz == MZ
+        and plan.kz * 2 == 8
+        and plan.no == 8
+        and plan.ky * MZ == LANES
+        and plan.t * plan.ky == plan.b
+        and plan.t * 2 * plan.ky * plan.kz == LANES
+        and plan.cy == groups * cols
+        and plan.cx % 8 == 0
+        and plan.a % 8 == 0
+    )
+    return plan if fits else None
+
+
 def solution(mesh):
+    def local(velocity, *weights):
+        plan = plan_of(mesh, velocity)
+        if plan is None:
+            return general(velocity, *weights)
+        return everyone(plan, velocity, *weights)
+
     return jax.shard_map(
         local,
         mesh=mesh,

time: 2110 us -> 245 us (0.12)
  waiting for transfers between devices: 741 us -> 57.1 us
  local copies, waits for them, and re-layouts: 642 us -> 10.8 us
  blocking collectives: 299 us -> 27.3 us
  other arithmetic: 165 us -> 1.66 us
  starting transfers between devices: 175 us -> 64.9 us
  Pallas kernels: 0 us -> 78.8 us
  loops' own time: 64.9 us -> 0 us
    all_gather x1 -> x0, waiting for transfers between devices: 383 us -> none  [local(): weights_full = lax.all_gather(spectral_weight, 'grp', axis=4, tiled=True)]
    unnamed x52 -> x67, local copies, waits for them, and re-layouts: 284 us -> 4.92 us
    psum x1 -> x0, blocking collectives: 264 us -> none  [local(): mix_total, loss_total = lax.psum((mix_term, loss_term), ('grp', 'py', 'pz'))]
    all_to_all x6 -> x5, waiting for transfers between devices: 235 us -> 43.4 us  [the longest x1 19.7 us: everyone(): spectra = lax.all_to_all(spectra, ('py', 'pz'), 0, 0, tiled=True)]
    reshape x2 -> x5, local copies, waits for them, and re-layouts: 154 us -> 0.4 us  [the longest x2 0.17 us: column(): value.reshape(3, G, plan.no).transpose(1, 0, 2).reshape(G * 3, plan.no, 1)]
    ppermute x18, starting transfers between devices: 145 us -> 39.9 us  [the longest x9 28.2 us: halos(): out.append(lax.ppermute(high, axis, up))]
    unnamed x3 -> x0, waiting for transfers between devices: 82.3 us -> none
    pallas_call x0 -> x10, Pallas kernels: none -> 78.8 us  [the longest x1 15.8 us: everyone(): pl.pallas_call(bind(mix_kernel), grid=(plan.a,), in_specs=[pl.BlockSpec((...]
  transfers between devices with their start and end apart: 26 -> 23, of which waited for: 19 -> 10; matrix products, arithmetic and copies ran while one was open for 19% -> 2% of each run, Pallas kernels for 0% -> 10%
where the time goes in v1:
time: 245 us; the launch traced here: 244 us
  Pallas kernels  78.8 us (32%)
  starting transfers between devices  64.9 us (26%)
  waiting for transfers between devices  57.1 us (23%)
  blocking collectives  27.3 us (11%)
  local copies, waits for them, and re-layouts  10.8 us (4%)
  between operations  2.97 us (1%)
    ppermute x9, starting transfers between devices, halos(): out.append(lax.ppermute(high, axis, up))  28.2 us
    all_to_all x1, waiting for transfers between devices, everyone(): spectra = lax.all_to_all(spectra, ('py', 'pz'), 0, 0, tiled=True)  19.7 us
    all_to_all x1, blocking collectives, everyone(): back = lax.all_to_all(back, ALL, 0, 0, tiled=True)  16.7 us
    pallas_call x1, Pallas kernels, everyone(): pl.pallas_call(bind(mix_kernel), grid=(plan.a,), in_specs=[pl.BlockSpec((...  15.8 us
    pallas_call x1, Pallas kernels, everyone(): pl.pallas_call(bind(grad_kernel), grid=(plan.a,), in_specs=[pl.BlockSpec(...  14.4 us
    ppermute x9, waiting for transfers between devices, halos(): out.append(lax.ppermute(low, axis, [(j, i) for i, j in up]))  13.5 us
    all_to_all x1, waiting for transfers between devices, everyone(): modes = lax.all_to_all(modes, ALL, 0, 0, tiled=True)  13.1 us
    ppermute x9, starting transfers between devices, halos(): out.append(lax.ppermute(low, axis, [(j, i) for i, j in up]))  11.6 us
  transfers between devices with their start and end apart: 23, of which 10 were waited for; matrix products, arithmetic and copies ran while one was open for 2% of the time, Pallas kernels for 10%

profile of v1, /device:TPU:0, one launch (start us, length us, event | category | flops | bytes accessed | tf_op | source)
XLA Modules:
  0.0 243.8 jit_solution(15951768484903037864)
XLA Ops:
  0.7 4.5 %shard_map.210 = (f32[72,512]{1,0:T(8,128)}, f32[48,128]{1,0:T(8,128)}, f32[48,128]{1,0:T(8,128)}, f32[144,128]{1,0:T(8,128)}, f32[144,128]{1,0:T(8,128)}, /*index=5*/f32[48,128]{1,0:T(8,128)}, f32[48,128]{1,0:T(8,128)}) custom-call(f32[2304,128]{1,0:T(8,128)} %bitcast.36, f32[2,128,128]{2,1,0:T(8,128)} %constant.64.clone.refs_1_.refs_9_), custom_call_target="tpu_custom_call" | custom-call | tf_op jit(solution)/shard_map/pallas_call | solution.py:787
  5.2 10.6 %all-gather = f32[288,512]{1,0:T(8,128)} all-gather(f32[72,512]{1,0:T(8,128)} %get-tuple-element.52), channel_id=2, replica_groups=mesh['grp'=4,'py'=4,'pz'=2] {'grp'}, dimensions={0}, use_global_device_ids=true | all-gather | bytes 737280 | tf_op jit(solution)/shard_map/all_gather | solution.py:792
  18.0 5.6 %shard_map.214 = f32[8,192,128]{2,1,0:T(8,128)} custom-call(f32[4,72,512]{2,1,0:T(8,128)} %bitcast.41, f32[64,72]{1,0:T(8,128)} %constant.67.clone.refs_1_, f32[2,2,128,128]{3,2,1,0:T(8,128)} %dynamic-slice_bitcast_fusion.refs_2_, f32[2,64,128]{2,1,0:T(8,128)} %dynamic-slice_bitcast_fusion.1.refs_3_), custom_call_target="tpu_custom_call" | custom-call | tf_op jit(solution)/shard_map/pallas_call | solution.py:796
  23.6 5.9 %all-to-all-start = ((f32[8,192,128]{2,1,0:T(8,128)}), f32[8,192,128]{2,1,0:T(8,128)S(1)}, u32[]{:S(2)}, u32[]{:S(2)}) async-start(f32[8,192,128]{2,1,0:T(8,128)} %shard_map.214), calls=%async_computation | async-start | bytes 1572864 | tf_op jit(solution)/shard_map/all_to_all | solution.py:800
  30.5 19.7 %all-to-all-done.refs_0_ = f32[8,192,128]{2,1,0:T(8,128)S(1)} async-done(((f32[8,192,128]{2,1,0:T(8,128)}), f32[8,192,128]{2,1,0:T(8,128)S(1)}, u32[]{:S(2)}, u32[]{:S(2)}) %all-to-all-start) | async-done | bytes 786464 | tf_op jit(solution)/shard_map/all_to_all | solution.py:800
  51.1 15.8 %shard_map.215 = (f32[8,2,32,256]{3,2,1,0:T(8,128)}, bf16[32,64,128]{2,1,0:T(8,128)(2,1)}) custom-call(f32[8,192,128]{2,1,0:T(8,128)} %copy-done.2, f32[12,256]{1,0:T(8,128)} %tile.12.refs_1_, f32[8,16,32,2,8,32]{5,4,3,2,1,0:T(8,128)} %refs_2_.4), custom_call_target="tpu_custom_call" | custom-call | tf_op jit(solution)/shard_map/pallas_call | solution.py:811
  66.8 2.7 %all-to-all-start.1 = ((bf16[32,64,128]{2,1,0:T(8,128)(2,1)}), bf16[32,64,128]{2,1,0:T(8,128)(2,1)S(1)}, u32[]{:S(2)}, u32[]{:S(2)}) async-start(bf16[32,64,128]{2,1,0:T(8,128)(2,1)} %get-tuple-element.54), calls=%async_computation.1 | async-start | bytes 1048576 | tf_op jit(solution)/shard_map/all_to_all | solution.py:830
  69.6 3.7 %collective-permute-start.2 = (f32[144,128]{1,0:T(8,128)S(1)}, f32[144,128]{1,0:T(8,128)S(1)}, u32[]{:S(2)}, u32[]{:S(2)}) collective-permute-start(f32[144,128]{1,0:T(8,128)S(1)} %copy-done.28), channel_id=1, source_target_pairs={{0,2},{2,4},{4,6},{1,3},{3,5},{5,7},{8,10},{10,12},{12,14},{9,11},... | collective-permute-start | bytes 221192 | tf_op jit(solution)/shard_map/ppermute | solution.py:767
  74.6 1.7 collective-permute-start
  77.7 3.4 %collective-permute-start.4 = (f32[48,128]{1,0:T(8,128)S(1)}, f32[48,128]{1,0:T(8,128)S(1)}, u32[]{:S(2)}, u32[]{:S(2)}) collective-permute-start(f32[48,128]{1,0:T(8,128)S(1)} %copy-done.30), channel_id=1, source_target_pairs={{0,1},{2,3},{4,5},{6,7},{8,9},{10,11},{12,13},{14,15},{16,17},{18,... | collective-permute-start | bytes 73736 | tf_op jit(solution)/shard_map/ppermute | solution.py:767
  82.5 4.2 %collective-permute-done.5.refs_7_ = f32[48,128]{1,0:T(8,128)S(1)} collective-permute-done((f32[48,128]{1,0:T(8,128)S(1)}, f32[48,128]{1,0:T(8,128)S(1)}, u32[]{:S(2)}, u32[]{:S(2)}) %collective-permute-start.5) | collective-permute-done | bytes 24608 | tf_op jit(solution)/shard_map/ppermute | solution.py:768
  88.1 6.4 %shard_map.211 = (f32[2304,128]{1,0:T(8,128)}, f32[48,128]{1,0:T(8,128)}, f32[48,128]{1,0:T(8,128)}, f32[144,128]{1,0:T(8,128)}, f32[144,128]{1,0:T(8,128)}, /*index=5*/f32[48,128]{1,0:T(8,128)}, f32[48,128]{1,0:T(8,128)}) custom-call(f32[2304,128]{1,0:T(8,128)} %bitcast.37, f32[2304,128]{1,0:T(8,128)} %bitcast.38, f32[48,128]{1,0:T(8,128)} %copy-done.15, ...), custom_call_target="tpu_custom_call" | custom-call | tf_op jit(solution)/shard_map/pallas_call | solution.py:840
  94.4 4.3 %collective-permute-start.8 = (f32[144,128]{1,0:T(8,128)}, f32[144,128]{1,0:T(8,128)S(1)}, u32[]{:S(2)}, u32[]{:S(2)}) collective-permute-start(f32[144,128]{1,0:T(8,128)} %get-tuple-element.40), channel_id=1, source_target_pairs={{0,2},{2,4},{4,6},{1,3},{3,5},{5,7},{8,10},{10,12},{12,14},{9,11},... | collective-permute-start | bytes 221192 | tf_op jit(solution)/shard_map/ppermute | solution.py:767
  100.0 2.9 %collective-permute-start.6 = (f32[48,128]{1,0:T(8,128)}, f32[48,128]{1,0:T(8,128)S(1)}, u32[]{:S(2)}, u32[]{:S(2)}) collective-permute-start(f32[48,128]{1,0:T(8,128)} %get-tuple-element.38), channel_id=1, source_target_pairs={{0,8},{8,16},{1,9},{9,17},{2,10},{10,18},{3,11},{11,19},{4,12},{12... | collective-permute-start | bytes 73736 | tf_op jit(solution)/shard_map/ppermute | solution.py:767
  104.2 1.9 collective-permute-start.10
  109.1 2.9 %collective-permute-done.11.refs_7_ = f32[48,128]{1,0:T(8,128)S(1)} collective-permute-done((f32[48,128]{1,0:T(8,128)}, f32[48,128]{1,0:T(8,128)S(1)}, u32[]{:S(2)}, u32[]{:S(2)}) %collective-permute-start.11) | collective-permute-done | bytes 24608 | tf_op jit(solution)/shard_map/ppermute | solution.py:768
  112.7 6.4 %shard_map.212 = (f32[2304,128]{1,0:T(8,128)}, f32[48,128]{1,0:T(8,128)}, f32[48,128]{1,0:T(8,128)}, f32[144,128]{1,0:T(8,128)}, f32[144,128]{1,0:T(8,128)}, /*index=5*/f32[48,128]{1,0:T(8,128)}, f32[48,128]{1,0:T(8,128)}) custom-call(f32[2304,128]{1,0:T(8,128)} %get-tuple-element.37.refs_0_, f32[2304,128]{1,0:T(8,128)} %bitcast.39, f32[48,128]{1,0:T(8,128)} %copy-done.14, ...), custom_call_target="tpu_custom_call" | custom-call | tf_op jit(solution)/shard_map/pallas_call | solution.py:844
  119.1 4.3 %collective-permute-start.14 = (f32[144,128]{1,0:T(8,128)}, f32[144,128]{1,0:T(8,128)S(1)}, u32[]{:S(2)}, u32[]{:S(2)}) collective-permute-start(f32[144,128]{1,0:T(8,128)} %get-tuple-element.47), channel_id=1, source_target_pairs={{0,2},{2,4},{4,6},{1,3},{3,5},{5,7},{8,10},{10,12},{12,14},{9,11},... | collective-permute-start | bytes 221192 | tf_op jit(solution)/shard_map/ppermute | solution.py:767
  124.7 4.3 %collective-permute-start.12 = (f32[48,128]{1,0:T(8,128)}, f32[48,128]{1,0:T(8,128)S(1)}, u32[]{:S(2)}, u32[]{:S(2)}) collective-permute-start(f32[48,128]{1,0:T(8,128)} %get-tuple-element.45), channel_id=1, source_target_pairs={{0,8},{8,16},{1,9},{9,17},{2,10},{10,18},{3,11},{11,19},{4,12},{12... | collective-permute-start | bytes 73736 | tf_op jit(solution)/shard_map/ppermute | solution.py:767
  130.2 1.9 collective-permute-start.16
  135.2 2.9 %collective-permute-done.17.refs_8_ = f32[48,128]{1,0:T(8,128)S(1)} collective-permute-done((f32[48,128]{1,0:T(8,128)}, f32[48,128]{1,0:T(8,128)S(1)}, u32[]{:S(2)}, u32[]{:S(2)}) %collective-permute-start.17) | collective-permute-done | bytes 24608 | tf_op jit(solution)/shard_map/ppermute | solution.py:768
  138.8 7.1 %shard_map.213 = (f32[2304,128]{1,0:T(8,128)}, bf16[8,72,128]{2,1,0:T(8,128)(2,1)}) custom-call(s32[1]{0:T(128)} %bitcast.refs_0_, f32[2304,128]{1,0:T(8,128)} %get-tuple-element.44.refs_1_, f32[2304,128]{1,0:T(8,128)} %bitcast.40, f32[48,128]{1,0:T(8,128)} %copy-done.13, f32[48,128]{1,0:T(8,128)} %copy-done.16, f32[144,128]{1,0:T(8,128)} %copy-done.7, ...), custom_call_target="tpu_custom_call" | custom-call | tf_op jit(solution)/shard_map/pallas_call | solution.py:851
  145.9 6.7 %all-to-all-start.3 = ((bf16[8,72,128]{2,1,0:T(8,128)(2,1)}), bf16[8,72,128]{2,1,0:T(8,128)(2,1)S(1)}, u32[]{:S(2)}, u32[]{:S(2)}) async-start(bf16[8,72,128]{2,1,0:T(8,128)(2,1)} %get-tuple-element.55), calls=%async_computation.3 | async-start | bytes 294912 | tf_op jit(solution)/shard_map/all_to_all | solution.py:859
  152.6 5.1 %shard_map.216 = bf16[32,40,128]{2,1,0:T(8,128)(2,1)} custom-call(bf16[32,64,128]{2,1,0:T(8,128)(2,1)} %copy-done.4, f32[256,256]{1,0:T(8,128)} %constant.68.clone.refs_1_.refs_3_, f32[256,256]{1,0:T(8,128)} %constant.69.clone.refs_2_.refs_4_, f32[256,640]{1,0:T(8,128)} %constant.70.clone.refs_3_, f32[256,640]{1,0:T(8,128)} %constant.71.clone.refs_4_), custom_call_target="tpu_custom_call" | custom-call | tf_op jit(solution)/shard_map/pallas_call | solution.py:833
  157.9 7.1 %all-to-all-start.2 = ((bf16[32,40,128]{2,1,0:T(8,128)(2,1)}), bf16[32,40,128]{2,1,0:T(8,128)(2,1)S(1)}, u32[]{:S(2)}, u32[]{:S(2)}) async-start(bf16[32,40,128]{2,1,0:T(8,128)(2,1)} %shard_map.216), calls=%async_computation.2 | async-start | bytes 655360 | tf_op jit(solution)/shard_map/all_to_all | solution.py:838
  166.5 10.5 %all-to-all-done.2.refs_0_ = bf16[32,40,128]{2,1,0:T(8,128)(2,1)S(1)} async-done(((bf16[32,40,128]{2,1,0:T(8,128)(2,1)}), bf16[32,40,128]{2,1,0:T(8,128)(2,1)S(1)}, u32[]{:S(2)}, u32[]{:S(2)}) %all-to-all-start.2) | async-done | bytes 327712 | tf_op jit(solution)/shard_map/all_to_all | solution.py:838
  178.4 7.7 %shard_map.217 = bf16[32,48,128]{2,1,0:T(8,128)(2,1)} custom-call(bf16[32,40,128]{2,1,0:T(8,128)(2,1)} %copy-done.5, f32[2,3,80,1,128]{4,3,2,1,0:T(1,128)} %bitcast.42, f32[64,128]{1,0:T(8,128)} %constant.72.clone.refs_2_, f32[64,128]{1,0:T(8,128)} %constant.73.clone.refs_3_, f32[12,8,128]{2,1,0:T(8,128)} %broadcast_in_dim.29.refs_4_, ...), custom_call_target="tpu_custom_call" | custom-call | tf_op jit(solution)/shard_map/pallas_call | solution.py:870
  186.1 16.7 %all_to_all.30.refs_0_ = bf16[32,48,128]{2,1,0:T(8,128)(2,1)} all-to-all(bf16[32,48,128]{2,1,0:T(8,128)(2,1)} %shard_map.217), channel_id=1, replica_groups=mesh['grp'=4,'py'=4,'pz'=2] {'grp','py','pz'}, dimensions={0} | all-to-all | bytes 786432 | tf_op jit(solution)/shard_map/all_to_all | solution.py:875
  202.8 5.8 %shard_map.218 = (bf16[32,64,128]{2,1,0:T(8,128)(2,1)}, f32[8,128]{1,0:T(8,128)}) custom-call(bf16[32,48,128]{2,1,0:T(8,128)(2,1)} %all_to_all.30.refs_0_, f32[256,640]{1,0:T(8,128)} %constant.74.clone.refs_1_, f32[256,640]{1,0:T(8,128)} %constant.75.clone.refs_2_, f32[256,256]{1,0:T(8,128)} %constant.68.clone.refs_1_.refs_3_, ...), custom_call_target="tpu_custom_call" | custom-call | tf_op jit(solution)/shard_map/pallas_call | solution.py:877
  208.6 2.6 %all-to-all-start.5 = ((bf16[32,64,128]{2,1,0:T(8,128)(2,1)}), bf16[32,64,128]{2,1,0:T(8,128)(2,1)S(1)}, u32[]{:S(2)}, u32[]{:S(2)}) async-start(bf16[32,64,128]{2,1,0:T(8,128)(2,1)} %get-tuple-element.56), calls=%async_computation.5 | async-start | bytes 1048576 | tf_op jit(solution)/shard_map/all_to_all | solution.py:882
  214.4 13.1 %all-to-all-done.5.refs_1_ = bf16[32,64,128]{2,1,0:T(8,128)(2,1)S(1)} async-done(((bf16[32,64,128]{2,1,0:T(8,128)(2,1)}), bf16[32,64,128]{2,1,0:T(8,128)(2,1)S(1)}, u32[]{:S(2)}, u32[]{:S(2)}) %all-to-all-start.5) | async-done | bytes 524320 | tf_op jit(solution)/shard_map/all_to_all | solution.py:882
  228.3 14.4 %shard_map.219 = f32[8,16,32,2,8,32]{5,4,3,2,1,0:T(8,128)} custom-call(f32[8,2,32,256]{3,2,1,0:T(8,128)} %get-tuple-element.53.refs_0_, bf16[32,64,128]{2,1,0:T(8,128)(2,1)} %copy-done.3), custom_call_target="tpu_custom_call" | custom-call | tf_op jit(solution)/shard_map/pallas_call | solution.py:884
  (124 shorter events, 28.2 us)
Async XLA Ops:
  0.6 164.3 %copy-start = (f32[32,32]{1,0:T(8,128)S(1)}, f32[32,32]{1,0:T(8,128)}, u32[]{:S(2)}) copy-start(f32[32,32]{1,0:T(8,128)} %param.22) | copy-start | bytes 12292
  0.6 15.2 %copy-start.6 = (f32[2,2,2,128,128]{4,3,2,1,0:T(8,128)S(1)}, f32[2,2,2,128,128]{4,3,2,1,0:T(8,128)}, u32[]{:S(2)}) copy-start(f32[2,2,2,128,128]{4,3,2,1,0:T(8,128)} %constant.65.clone) | copy-start | bytes 1572868
  23.6 26.6 %all-to-all-start = ((f32[8,192,128]{2,1,0:T(8,128)}), f32[8,192,128]{2,1,0:T(8,128)S(1)}, u32[]{:S(2)}, u32[]{:S(2)}) async-start(f32[8,192,128]{2,1,0:T(8,128)} %shard_map.214), calls=%async_computation | async-start | bytes 1572864 | tf_op jit(solution)/shard_map/all_to_all | solution.py:800
  30.4 39.1 %copy-start.28 = (f32[144,128]{1,0:T(8,128)S(1)}, f32[144,128]{1,0:T(8,128)}, u32[]{:S(2)}) copy-start(f32[144,128]{1,0:T(8,128)} %get-tuple-element.33) | copy-start | bytes 221188
  30.4 42.8 %copy-start.27 = (f32[144,128]{1,0:T(8,128)S(1)}, f32[144,128]{1,0:T(8,128)}, u32[]{:S(2)}) copy-start(f32[144,128]{1,0:T(8,128)} %get-tuple-element.34) | copy-start | bytes 221188
  30.4 44.1 %copy-start.32 = (f32[48,128]{1,0:T(8,128)S(1)}, f32[48,128]{1,0:T(8,128)}, u32[]{:S(2)}) copy-start(f32[48,128]{1,0:T(8,128)} %get-tuple-element.31) | copy-start | bytes 73732
  30.4 45.9 %copy-start.31 = (f32[48,128]{1,0:T(8,128)S(1)}, f32[48,128]{1,0:T(8,128)}, u32[]{:S(2)}) copy-start(f32[48,128]{1,0:T(8,128)} %get-tuple-element.32) | copy-start | bytes 73732
  30.4 47.2 %copy-start.30 = (f32[48,128]{1,0:T(8,128)S(1)}, f32[48,128]{1,0:T(8,128)}, u32[]{:S(2)}) copy-start(f32[48,128]{1,0:T(8,128)} %get-tuple-element.35) | copy-start | bytes 73732
  30.5 50.6 %copy-start.29 = (f32[48,128]{1,0:T(8,128)S(1)}, f32[48,128]{1,0:T(8,128)}, u32[]{:S(2)}) copy-start(f32[48,128]{1,0:T(8,128)} %get-tuple-element.36) | copy-start | bytes 73732
  66.8 79.1 %all-to-all-start.1 = ((bf16[32,64,128]{2,1,0:T(8,128)(2,1)}), bf16[32,64,128]{2,1,0:T(8,128)(2,1)S(1)}, u32[]{:S(2)}, u32[]{:S(2)}) async-start(bf16[32,64,128]{2,1,0:T(8,128)(2,1)} %get-tuple-element.54), calls=%async_computation.1 | async-start | bytes 1048576 | tf_op jit(solution)/shard_map/all_to_all | solution.py:830
  69.6 17.2 %collective-permute-start.2 = (f32[144,128]{1,0:T(8,128)S(1)}, f32[144,128]{1,0:T(8,128)S(1)}, u32[]{:S(2)}, u32[]{:S(2)}) collective-permute-start(f32[144,128]{1,0:T(8,128)S(1)} %copy-done.28), channel_id=1, source_target_pairs={{0,2},{2,4},{4,6},{1,3},{3,5},{5,7},{8,10},{10,12},{12,14},{9,11},... | collective-permute-start | bytes 221192 | tf_op jit(solution)/shard_map/ppermute | solution.py:767
  73.3 13.5 %collective-permute-start.3 = (f32[144,128]{1,0:T(8,128)S(1)}, f32[144,128]{1,0:T(8,128)S(1)}, u32[]{:S(2)}, u32[]{:S(2)}) collective-permute-start(f32[144,128]{1,0:T(8,128)S(1)} %copy-done.27), channel_id=1, source_target_pairs={{2,0},{4,2},{6,4},{3,1},{5,3},{7,5},{10,8},{12,10},{14,12},{11,9},... | collective-permute-start | bytes 221192 | tf_op jit(solution)/shard_map/ppermute | solution.py:768
  74.6 6.4 %collective-permute-start = (f32[48,128]{1,0:T(8,128)S(1)}, f32[48,128]{1,0:T(8,128)S(1)}, u32[]{:S(2)}, u32[]{:S(2)}) collective-permute-start(f32[48,128]{1,0:T(8,128)S(1)} %copy-done.32), channel_id=1, source_target_pairs={{0,8},{8,16},{1,9},{9,17},{2,10},{10,18},{3,11},{11,19},{4,12},{12... | collective-permute-start | bytes 73736 | tf_op jit(solution)/shard_map/ppermute | solution.py:767
  76.4 6.0 %collective-permute-start.1 = (f32[48,128]{1,0:T(8,128)S(1)}, f32[48,128]{1,0:T(8,128)S(1)}, u32[]{:S(2)}, u32[]{:S(2)}) collective-permute-start(f32[48,128]{1,0:T(8,128)S(1)} %copy-done.31), channel_id=1, source_target_pairs={{8,0},{16,8},{9,1},{17,9},{10,2},{18,10},{11,3},{19,11},{12,4},{20... | collective-permute-start | bytes 73736 | tf_op jit(solution)/shard_map/ppermute | solution.py:768
  77.7 4.9 %collective-permute-start.4 = (f32[48,128]{1,0:T(8,128)S(1)}, f32[48,128]{1,0:T(8,128)S(1)}, u32[]{:S(2)}, u32[]{:S(2)}) collective-permute-start(f32[48,128]{1,0:T(8,128)S(1)} %copy-done.30), channel_id=1, source_target_pairs={{0,1},{2,3},{4,5},{6,7},{8,9},{10,11},{12,13},{14,15},{16,17},{18,... | collective-permute-start | bytes 73736 | tf_op jit(solution)/shard_map/ppermute | solution.py:767
  81.1 5.7 %collective-permute-start.5 = (f32[48,128]{1,0:T(8,128)S(1)}, f32[48,128]{1,0:T(8,128)S(1)}, u32[]{:S(2)}, u32[]{:S(2)}) collective-permute-start(f32[48,128]{1,0:T(8,128)S(1)} %copy-done.29), channel_id=1, source_target_pairs={{1,0},{3,2},{5,4},{7,6},{9,8},{11,10},{13,12},{15,14},{17,16},{19,... | collective-permute-start | bytes 73736 | tf_op jit(solution)/shard_map/ppermute | solution.py:768
  94.4 17.6 %collective-permute-start.8 = (f32[144,128]{1,0:T(8,128)}, f32[144,128]{1,0:T(8,128)S(1)}, u32[]{:S(2)}, u32[]{:S(2)}) collective-permute-start(f32[144,128]{1,0:T(8,128)} %get-tuple-element.40), channel_id=1, source_target_pairs={{0,2},{2,4},{4,6},{1,3},{3,5},{5,7},{8,10},{10,12},{12,14},{9,11},... | collective-permute-start | bytes 221192 | tf_op jit(solution)/shard_map/ppermute | solution.py:767
  98.7 13.3 %collective-permute-start.9 = (f32[144,128]{1,0:T(8,128)}, f32[144,128]{1,0:T(8,128)S(1)}, u32[]{:S(2)}, u32[]{:S(2)}) collective-permute-start(f32[144,128]{1,0:T(8,128)} %get-tuple-element.41), channel_id=1, source_target_pairs={{2,0},{4,2},{6,4},{3,1},{5,3},{7,5},{10,8},{12,10},{14,12},{11,9},... | collective-permute-start | bytes 221192 | tf_op jit(solution)/shard_map/ppermute | solution.py:768
  100.0 6.1 %collective-permute-start.6 = (f32[48,128]{1,0:T(8,128)}, f32[48,128]{1,0:T(8,128)S(1)}, u32[]{:S(2)}, u32[]{:S(2)}) collective-permute-start(f32[48,128]{1,0:T(8,128)} %get-tuple-element.38), channel_id=1, source_target_pairs={{0,8},{8,16},{1,9},{9,17},{2,10},{10,18},{3,11},{11,19},{4,12},{12... | collective-permute-start | bytes 73736 | tf_op jit(solution)/shard_map/ppermute | solution.py:767
  102.9 6.2 %collective-permute-start.7 = (f32[48,128]{1,0:T(8,128)}, f32[48,128]{1,0:T(8,128)S(1)}, u32[]{:S(2)}, u32[]{:S(2)}) collective-permute-start(f32[48,128]{1,0:T(8,128)} %get-tuple-element.39), channel_id=1, source_target_pairs={{8,0},{16,8},{9,1},{17,9},{10,2},{18,10},{11,3},{19,11},{12,4},{20... | collective-permute-start | bytes 73736 | tf_op jit(solution)/shard_map/ppermute | solution.py:768
  104.2 5.0 %collective-permute-start.10 = (f32[48,128]{1,0:T(8,128)}, f32[48,128]{1,0:T(8,128)S(1)}, u32[]{:S(2)}, u32[]{:S(2)}) collective-permute-start(f32[48,128]{1,0:T(8,128)} %get-tuple-element.42), channel_id=1, source_target_pairs={{0,1},{2,3},{4,5},{6,7},{8,9},{10,11},{12,13},{14,15},{16,17},{18,... | collective-permute-start | bytes 73736 | tf_op jit(solution)/shard_map/ppermute | solution.py:767
  106.1 5.9 %collective-permute-start.11 = (f32[48,128]{1,0:T(8,128)}, f32[48,128]{1,0:T(8,128)S(1)}, u32[]{:S(2)}, u32[]{:S(2)}) collective-permute-start(f32[48,128]{1,0:T(8,128)} %get-tuple-element.43), channel_id=1, source_target_pairs={{1,0},{3,2},{5,4},{7,6},{9,8},{11,10},{13,12},{15,14},{17,16},{19,... | collective-permute-start | bytes 73736 | tf_op jit(solution)/shard_map/ppermute | solution.py:768
  119.1 19.0 %collective-permute-start.14 = (f32[144,128]{1,0:T(8,128)}, f32[144,128]{1,0:T(8,128)S(1)}, u32[]{:S(2)}, u32[]{:S(2)}) collective-permute-start(f32[144,128]{1,0:T(8,128)} %get-tuple-element.47), channel_id=1, source_target_pairs={{0,2},{2,4},{4,6},{1,3},{3,5},{5,7},{8,10},{10,12},{12,14},{9,11},... | collective-permute-start | bytes 221192 | tf_op jit(solution)/shard_map/ppermute | solution.py:767
  123.4 14.7 %collective-permute-start.15 = (f32[144,128]{1,0:T(8,128)}, f32[144,128]{1,0:T(8,128)S(1)}, u32[]{:S(2)}, u32[]{:S(2)}) collective-permute-start(f32[144,128]{1,0:T(8,128)} %get-tuple-element.48), channel_id=1, source_target_pairs={{2,0},{4,2},{6,4},{3,1},{5,3},{7,5},{10,8},{12,10},{14,12},{11,9},... | collective-permute-start | bytes 221192 | tf_op jit(solution)/shard_map/ppermute | solution.py:768
  124.7 7.5 %collective-permute-start.12 = (f32[48,128]{1,0:T(8,128)}, f32[48,128]{1,0:T(8,128)S(1)}, u32[]{:S(2)}, u32[]{:S(2)}) collective-permute-start(f32[48,128]{1,0:T(8,128)} %get-tuple-element.45), channel_id=1, source_target_pairs={{0,8},{8,16},{1,9},{9,17},{2,10},{10,18},{3,11},{11,19},{4,12},{12... | collective-permute-start | bytes 73736 | tf_op jit(solution)/shard_map/ppermute | solution.py:767
  128.9 6.2 %collective-permute-start.13 = (f32[48,128]{1,0:T(8,128)}, f32[48,128]{1,0:T(8,128)S(1)}, u32[]{:S(2)}, u32[]{:S(2)}) collective-permute-start(f32[48,128]{1,0:T(8,128)} %get-tuple-element.46), channel_id=1, source_target_pairs={{8,0},{16,8},{9,1},{17,9},{10,2},{18,10},{11,3},{19,11},{12,4},{20... | collective-permute-start | bytes 73736 | tf_op jit(solution)/shard_map/ppermute | solution.py:768
  130.2 5.0 %collective-permute-start.16 = (f32[48,128]{1,0:T(8,128)}, f32[48,128]{1,0:T(8,128)S(1)}, u32[]{:S(2)}, u32[]{:S(2)}) collective-permute-start(f32[48,128]{1,0:T(8,128)} %get-tuple-element.49), channel_id=1, source_target_pairs={{0,1},{2,3},{4,5},{6,7},{8,9},{10,11},{12,13},{14,15},{16,17},{18,... | collective-permute-start | bytes 73736 | tf_op jit(solution)/shard_map/ppermute | solution.py:767
  132.2 5.9 %collective-permute-start.17 = (f32[48,128]{1,0:T(8,128)}, f32[48,128]{1,0:T(8,128)S(1)}, u32[]{:S(2)}, u32[]{:S(2)}) collective-permute-start(f32[48,128]{1,0:T(8,128)} %get-tuple-element.50), channel_id=1, source_target_pairs={{1,0},{3,2},{5,4},{7,6},{9,8},{11,10},{13,12},{15,14},{17,16},{19,... | collective-permute-start | bytes 73736 | tf_op jit(solution)/shard_map/ppermute | solution.py:768
  145.9 12.0 %all-to-all-start.3 = ((bf16[8,72,128]{2,1,0:T(8,128)(2,1)}), bf16[8,72,128]{2,1,0:T(8,128)(2,1)S(1)}, u32[]{:S(2)}, u32[]{:S(2)}) async-start(bf16[8,72,128]{2,1,0:T(8,128)(2,1)} %get-tuple-element.55), calls=%async_computation.3 | async-start | bytes 294912 | tf_op jit(solution)/shard_map/all_to_all | solution.py:859
  157.9 19.1 %all-to-all-start.2 = ((bf16[32,40,128]{2,1,0:T(8,128)(2,1)}), bf16[32,40,128]{2,1,0:T(8,128)(2,1)S(1)}, u32[]{:S(2)}, u32[]{:S(2)}) async-start(bf16[32,40,128]{2,1,0:T(8,128)(2,1)} %shard_map.216), calls=%async_computation.2 | async-start | bytes 655360 | tf_op jit(solution)/shard_map/all_to_all | solution.py:838
  208.6 18.8 %all-to-all-start.5 = ((bf16[32,64,128]{2,1,0:T(8,128)(2,1)}), bf16[32,64,128]{2,1,0:T(8,128)(2,1)S(1)}, u32[]{:S(2)}, u32[]{:S(2)}) async-start(bf16[32,64,128]{2,1,0:T(8,128)(2,1)} %get-tuple-element.56), calls=%async_computation.5 | async-start | bytes 1048576 | tf_op jit(solution)/shard_map/all_to_all | solution.py:882
  228.3 14.5 %copy-start.1 = (f32[32,32]{1,0:T(8,128)S(1)}, f32[32,32]{1,0:T(8,128)}, u32[]{:S(2)}) copy-start(f32[32,32]{1,0:T(8,128)} %param.22) | copy-start | bytes 12292
  (24 other events, 72.3 us)
